TPU v7x, 512 devices: a whole 4x8x8 slice. The times are simulated.
512 devices in a mesh: sp: 64 (over z_hi, y, core), ch: 8 (over z_lo, x).
Axes of the slice: x: 4, y: 8, z: 8 (z_hi: 4, z_lo: 2; z = z_hi * 2 + z_lo), core: 2. Of those that a mesh axis runs over, the one named last changes fastest.
Arguments:
- image: bfloat16 [64, 4, 64, 768], P('sp', None, None, 'ch'), may hold values from -60 to 60
- cotangent: bfloat16 [64, 4, 64, 768], P('sp', None, None, 'ch'), may hold values from -6 to 6
- kernel: bfloat16 [7, 7, 768], P(None, None, 'ch'), may hold values from -0.875 to 0.875
- w_in: bfloat16 [768, 3072], P(None, 'ch'), may hold values from -0.21875 to 0.21875
- w_out: bfloat16 [3072, 768], P('ch'), may hold values from -0.109375 to 0.109375
Outputs:
- output: bfloat16 [64, 4, 64, 768], P('sp', None, None, 'ch')
- grad_image: bfloat16 [64, 4, 64, 768], P('sp', None, None, 'ch')
- grad_in: float32 [768, 3072], P(None, 'ch')
- grad_out: float32 [3072, 768], P('ch')
- grad_kernel: float32 [7, 7, 768], P(None, None, 'ch')
All inputs are finite; a program needn't handle non-finite values.
Results may differ from a plain program's by a relative error of at most 0.015.
Values may be sent and summed in bfloat16 or wider, within the bound.
A program may use at most 64 MiB of HBM per device.

v0:
```python
import jax
import jax.numpy as jnp
from jax import lax
from jax.sharding import PartitionSpec as P

GRID_W = 8


def passed_along(block, axis, distance):
    devices = range(lax.axis_size(axis))
    route = [(i - distance, i) for i in devices if i - distance in devices]
    return lax.ppermute(block, axis, route)


def from_peer(piece, offset):
    return passed_along(piece, "sp", offset)


def widen(block):
    column = lax.axis_index("sp") % GRID_W
    left = from_peer(block[:, -3:], 1)
    left = jnp.where(column == 0, jnp.zeros_like(left), left)
    right = from_peer(block[:, :3], -1)
    right = jnp.where(column == GRID_W - 1, jnp.zeros_like(right), right)
    wide = jnp.concatenate([left, block, right], axis=1)
    upper = from_peer(wide[-3:], GRID_W)
    lower = from_peer(wide[:3], -GRID_W)
    return jnp.concatenate([upper, wide, lower], axis=0)


def shards(image, cotangent, kernel, w_in, w_out):
    block = image[0]
    grad_map = cotangent[0]
    rows, cols, panel = block.shape
    chans = w_in.shape[0]
    kernel_f = kernel.astype(jnp.float32)
    padded = widen(block).astype(jnp.float32)
    total = jnp.zeros((rows, cols, panel), jnp.float32)
    for row in range(7):
        for col in range(7):
            total = total + kernel_f[row, col] * padded[row : row + rows, col : col + cols]
    conv = total.astype(jnp.bfloat16)
    conv_f = conv.astype(jnp.float32)
    first_sum, square_sum = lax.psum(
        (jnp.sum(conv_f, axis=-1, keepdims=True), jnp.sum(conv_f * conv_f, axis=-1, keepdims=True)),
        "ch",
    )
    mean = first_sum / chans
    var = square_sum / chans - mean * mean
    rstd = lax.rsqrt(var + 1e-06)
    normed_all = lax.all_gather(
        ((conv_f - mean) * rstd).astype(jnp.bfloat16), "ch", axis=2, tiled=True
    )
    local_hat = (conv_f - mean) * rstd
    pre = jnp.einsum("hwc,cf->hwf", normed_all, w_in, preferred_element_type=jnp.float32)
    act = (0.5 * pre * (1.0 + jax.scipy.special.erf(pre / jnp.sqrt(2.0)))).astype(jnp.bfloat16)
    partial_out = jnp.einsum("hwf,fc->hwc", act, w_out, preferred_element_type=jnp.float32).astype(
        jnp.bfloat16
    )
    branch = lax.psum_scatter(partial_out, "ch", scatter_dimension=2, tiled=True).astype(
        jnp.float32
    )
    output = (block.astype(jnp.float32) + branch).astype(jnp.bfloat16)
    grad_all = lax.all_gather(grad_map, "ch", axis=2, tiled=True)
    d_act = jnp.einsum("hwc,fc->hwf", grad_all, w_out, preferred_element_type=jnp.float32)
    grad_out = jnp.einsum("hwf,hwc->fc", act, grad_all, preferred_element_type=jnp.float32)
    slope = 0.5 * (1.0 + jax.scipy.special.erf(pre / jnp.sqrt(2.0))) + pre * jnp.exp(
        -0.5 * pre * pre
    ) / jnp.sqrt(2.0 * jnp.pi)
    d_pre = (d_act * slope).astype(jnp.bfloat16)
    grad_in = jnp.einsum("hwc,hwf->cf", normed_all, d_pre, preferred_element_type=jnp.float32)
    partial_norm = jnp.einsum(
        "hwf,cf->hwc", d_pre, w_in, preferred_element_type=jnp.float32
    ).astype(jnp.bfloat16)
    d_norm = lax.psum_scatter(partial_norm, "ch", scatter_dimension=2, tiled=True).astype(
        jnp.float32
    )
    first, second = lax.psum(
        (
            jnp.sum(d_norm, axis=-1, keepdims=True),
            jnp.sum(d_norm * local_hat, axis=-1, keepdims=True),
        ),
        "ch",
    )
    d_conv = (rstd * (d_norm - first / chans - local_hat * second / chans)).astype(jnp.bfloat16)
    d_conv_f = d_conv.astype(jnp.float32)
    taps = []
    for row in range(7):
        for col in range(7):
            taps.append(jnp.sum(d_conv_f * padded[row : row + rows, col : col + cols], axis=(0, 1)))
    grad_kernel = jnp.stack(taps).reshape(7, 7, panel)
    d_padded = widen(d_conv).astype(jnp.float32)
    back = grad_map.astype(jnp.float32)
    for row in range(7):
        for col in range(7):
            back = (
                back
                + kernel_f[row, col] * d_padded[6 - row : 6 - row + rows, 6 - col : 6 - col + cols]
            )
    grad_image = back.astype(jnp.bfloat16)
    grad_in, grad_out, grad_kernel = lax.psum((grad_in, grad_out, grad_kernel), "sp")
    return (output[None], grad_image[None], grad_in, grad_out, grad_kernel)


def solution(mesh):
    return jax.shard_map(
        shards,
        mesh=mesh,
        in_specs=(
            P("sp", None, None, "ch"),
            P("sp", None, None, "ch"),
            P(None, None, "ch"),
            P(None, "ch"),
            P("ch", None),
        ),
        out_specs=(
            P("sp", None, None, "ch"),
            P("sp", None, None, "ch"),
            P(None, "ch"),
            P("ch", None),
            P(None, None, "ch"),
        ),
        check_vma=False,
    )
```

profile of v0, /device:TPU:6, one launch (start us, length us, event | category | flops | bytes accessed | tf_op | source)
XLA Modules:
  0.0 716.1 jit_solution(15601981577770408222)
XLA Ops:
  8.1 1.0 copy.38
  9.2 1.7 collective-permute-start
  10.9 1.3 collective-permute-start.1
  12.2 0.7 convert_element_type.55
  13.4 0.6 slice_bitcast_fusion.46
  14.0 1.0 copy.42
  15.0 0.5 collective-permute-done.1
  15.9 11.0 %collective-permute-start.2 = (bf16[3,70,96]{1,0,2:T(4,128)(2,1)S(1)}, bf16[3,70,96]{1,0,2:T(4,128)(2,1)S(1)}, u32[]{:S(2)}, u32[]{:S(2)}) collective-permute-start(bf16[3,70,96]{1,0,2:T(4,128)(2,1)S(1)} %get-tuple-element.85), channel_id=1, source_target_pairs={{0,64},{8,72},{16,80},{24,88},{32,96},{40,104},{48,112},{56,120},{... | collective-permute-start | bytes 120968 | tf_op jit(solution)/shard_map/ppermute | solution.py:12
  26.9 1.3 collective-permute-start.3
  28.2 29.8 %all-gather = bf16[1,4,64,768]{2,1,0,3:T(4,128)(2,1)S(1)} all-gather(bf16[1,4,64,96]{2,1,0,3:T(4,128)(2,1)S(1)} %copy.42), channel_id=2, replica_groups=mesh['sp'=64,'ch'=8] {'ch'}, dimensions={3}, use_global_device_ids=true | all-gather | bytes 442368 | tf_op jit(solution)/shard_map/all_gather | solution.py:64
  58.0 0.5 copy.43
  58.6 0.7 maximum_convert_fusion
  59.6 12.5 %convert_reduce_fusion.1 = (f32[4,64]{1,0:T(4,128)S(1)}, f32[4,64]{1,0:T(4,128)S(1)}, bf16[4,64,96]{1,0,2:T(4,128)(2,1)S(1)}) fusion(f32[10,70,96]{1,0,2:T(8,128)S(1)} %maximum_convert_fusion, f32[96]{0:T(128)S(1)} %get-tuple-element.90, f32[96]{0:T(128)S(1)} %get-tuple-element.91, f32[96]{0:T(128)S(1)} %get-tuple-element.92, f32[96]{0:T(128)S(1)} %get-tuple-element.93, ...), kind=kLoop, calls=%fused_computation.76 | loop fusion | flops 2506240 | bytes 4886912 | tf_op jit(solution)/shard_map/reduce_sum | solution.py:45
  72.1 16.1 %all-reduce.2 = (f32[4,64,1]{1,0,2:T(4,128)S(1)}, f32[4,64,1]{1,0,2:T(4,128)S(1)}) all-reduce(f32[4,64,1]{1,0,2:T(4,128)S(1)} %bitcast.206, f32[4,64,1]{1,0,2:T(4,128)S(1)} %bitcast.205), channel_id=1, replica_groups=mesh['sp'=64,'ch'=8] {'ch'}, use_global_device_ids=true, to_apply=%region_3.4 | all-reduce | flops 512 | bytes 4096 | tf_op jit(solution)/shard_map/psum | solution.py:44
  88.4 29.7 %all_gather.6 = bf16[4,64,768]{1,0,2:T(4,128)(2,1)S(1)} all-gather(bf16[4,64,96]{1,0,2:T(4,128)(2,1)S(1)} %fusion.14), channel_id=1, replica_groups=mesh['sp'=64,'ch'=8] {'ch'}, dimensions={2}, use_global_device_ids=true | all-gather | bytes 442368 | tf_op jit(solution)/shard_map/all_gather | solution.py:51
  118.1 0.5 copy.39
  118.7 0.4 fusion.4
  119.0 0.7 copy-done.6
  119.7 0.4 fusion
  120.1 0.7 copy-done.4
  120.8 0.4 convolution_convert_fusion
  121.2 0.6 copy.50
  121.8 1.2 reshape.23
  123.1 1.4 convolution_convert_fusion.1
  124.5 0.6 copy.48
  125.1 1.2 reshape.21
  126.6 1.4 convolution_bitcast_fusion.1
  128.0 1.4 convolution_bitcast_fusion
  129.4 43.3 %reduce-scatter.9.cloned.1.call-done = bf16[96,256]{1,0:T(8,128)(2,1)} async-done(((bf16[768,256]{1,0:T(8,128)(2,1)}), bf16[96,256]{1,0:T(8,128)(2,1)}) %reduce-scatter.9.cloned.1.call-update) | async-done | bytes 49168
  172.7 0.9 reshape.24
  173.8 16.5 %all-reduce.1 = (f32[4,64]{1,0:T(4,128)S(1)}, f32[4,64,1]{1,0,2:T(4,128)S(1)}) all-reduce(f32[4,64]{1,0:T(4,128)S(1)} %get-tuple-element.70, f32[4,64,1]{1,0,2:T(4,128)S(1)} %bitcast.204), channel_id=1, replica_groups=mesh['sp'=64,'ch'=8] {'ch'}, use_global_device_ids=true, to_apply=%region_9.10 | all-reduce | flops 512 | bytes 4096 | tf_op jit(solution)/shard_map/psum | solution.py:78
  190.3 6.9 fusion.68
  197.2 4.6 fusion.67
  201.9 1.5 collective-permute-start.4
  203.5 6.7 fusion.69
  210.2 1.3 collective-permute-start.5
  211.5 7.1 reduce-scatter.7.cloned.1.call-done
  218.6 0.9 reshape.22
  220.3 6.4 collective-permute-start.6
  226.7 1.3 collective-permute-start.7
  228.1 0.7 copy.46
  229.0 282.1 %psum.55 = f32[7,7,96]{2,1,0:T(8,128)} all-reduce(f32[7,7,96]{2,1,0:T(8,128)S(1)} %reshape.13), channel_id=1, replica_groups=mesh['sp'=64,'ch'=8] {'sp'}, use_global_device_ids=true, to_apply=%region_61.62 | all-reduce | flops 4704 | bytes 37632 | tf_op jit(solution)/shard_map/psum | solution.py:101
  511.1 0.7 maximum_convert_fusion.1
  512.1 12.5 %fusion.121 = bf16[1,4,64,96]{2,1,3,0:T(4,128)(2,1)S(1)} fusion(f32[10,70,96]{1,0,2:T(8,128)S(1)} %maximum_convert_fusion.1, f32[96]{0:T(128)S(1)} %copy-done.45, f32[96]{0:T(128)S(1)} %copy-done.47, f32[96]{0:T(128)S(1)} %copy-done.49, f32[96]{0:T(128)S(1)} %copy-done.51, f32[96]{0:T(128)S(1)} %copy-done.53, f32[96]{0:T(128)S(1)} %copy-done.55, ...), kind=kLoop, calls=%fused_computation.243 | loop fusion | flops 2457600 | bytes 4934016 | tf_op jit(solution)/shard_map/broadcast_in_dim | solution.py:102
  524.6 0.7 copy.47
  525.3 179.9 %all-reduce.5.cloned.1.call-done = (f32[768,384]{1,0:T(8,128)}, f32[384,768]{1,0:T(8,128)}) async-done(((f32[768,384]{1,0:T(8,128)}, f32[384,768]{1,0:T(8,128)}), (f32[768,384]{1,0:T(8,128)}, f32[384,768]{1,0:T(8,128)})) %all-reduce.5.cloned.1.call-update) | async-done | bytes 2359312 | tf_op jit(solution)/shard_map/psum | solution.py:101
  705.2 2.5 copy.54
  707.6 1.0 copy.55
  (199 shorter events, 2.2 us)
Async XLA Ops:
  8.0 164.7 %reduce-scatter.9.cloned.1.call-start = ((), (), s32[]{:S(2)}) async-start(), calls=%async_computation.3 | async-start | bytes 442368
  9.2 5.8 collective-permute-start
  10.9 4.6 collective-permute-start.1
  15.9 42.7 %collective-permute-start.2 = (bf16[3,70,96]{1,0,2:T(4,128)(2,1)S(1)}, bf16[3,70,96]{1,0,2:T(4,128)(2,1)S(1)}, u32[]{:S(2)}, u32[]{:S(2)}) collective-permute-start(bf16[3,70,96]{1,0,2:T(4,128)(2,1)S(1)} %get-tuple-element.85), channel_id=1, source_target_pairs={{0,64},{8,72},{16,80},{24,88},{32,96},{40,104},{48,112},{56,120},{... | collective-permute-start | bytes 120968 | tf_op jit(solution)/shard_map/ppermute | solution.py:12
  26.9 31.7 %collective-permute-start.3 = (bf16[3,70,96]{1,0,2:T(4,128)(2,1)S(1)}, bf16[3,70,96]{1,0,2:T(4,128)(2,1)S(1)}, u32[]{:S(2)}, u32[]{:S(2)}) collective-permute-start(bf16[3,70,96]{1,0,2:T(4,128)(2,1)S(1)} %get-tuple-element.86), channel_id=1, source_target_pairs={{64,0},{72,8},{80,16},{88,24},{96,32},{104,40},{112,48},{120,56},{... | collective-permute-start | bytes 120968 | tf_op jit(solution)/shard_map/ppermute | solution.py:12
  123.0 95.5 %reduce-scatter.7.cloned.1.call-start = ((), (), s32[]{:S(2)}) async-start(), calls=%async_computation.2 | async-start | bytes 442368
  126.4 578.8 %all-reduce.5.cloned.1.call-start = ((), (), s32[]{:S(2)}) async-start(), calls=%async_computation.4 | async-start | bytes 4718592 | tf_op jit(solution)/shard_map/psum | solution.py:101
  201.9 17.5 %collective-permute-start.4 = (bf16[4,3,96]{1,0,2:T(4,128)(2,1)S(1)}, bf16[4,3,96]{1,0,2:T(4,128)(2,1)S(1)}, u32[]{:S(2)}, u32[]{:S(2)}) collective-permute-start(bf16[4,3,96]{1,0,2:T(4,128)(2,1)S(1)} %get-tuple-element.83), channel_id=1, source_target_pairs={{0,8},{8,16},{16,24},{24,32},{32,40},{40,48},{48,56},{56,64},{64,7... | collective-permute-start | bytes 6920 | tf_op jit(solution)/shard_map/ppermute | solution.py:12
  210.2 9.4 %collective-permute-start.5 = (bf16[4,3,96]{1,0,2:T(4,128)(2,1)S(1)}, bf16[4,3,96]{1,0,2:T(4,128)(2,1)S(1)}, u32[]{:S(2)}, u32[]{:S(2)}) collective-permute-start(bf16[4,3,96]{1,0,2:T(4,128)(2,1)S(1)} %get-tuple-element.84), channel_id=1, source_target_pairs={{8,0},{16,8},{24,16},{32,24},{40,32},{48,40},{56,48},{64,56},{72,6... | collective-permute-start | bytes 6920 | tf_op jit(solution)/shard_map/ppermute | solution.py:12
  219.8 291.9 %copy-start.9 = (f32[96]{0:T(128)S(1)}, f32[96]{0:T(128)}, u32[]{:S(2)}) copy-start(f32[96]{0:T(128)} %copy-done.8) | copy-start | bytes 1156
  219.8 291.9 %copy-start.11 = (f32[96]{0:T(128)S(1)}, f32[96]{0:T(128)}, u32[]{:S(2)}) copy-start(f32[96]{0:T(128)} %copy-done.10) | copy-start | bytes 1156
  219.8 291.9 %copy-start.13 = (f32[96]{0:T(128)S(1)}, f32[96]{0:T(128)}, u32[]{:S(2)}) copy-start(f32[96]{0:T(128)} %copy-done.12) | copy-start | bytes 1156
  219.9 291.9 %copy-start.15 = (f32[96]{0:T(128)S(1)}, f32[96]{0:T(128)}, u32[]{:S(2)}) copy-start(f32[96]{0:T(128)} %copy-done.14) | copy-start | bytes 1156
  219.9 291.9 %copy-start.17 = (f32[96]{0:T(128)S(1)}, f32[96]{0:T(128)}, u32[]{:S(2)}) copy-start(f32[96]{0:T(128)} %copy-done.16) | copy-start | bytes 1156
  219.9 291.9 %copy-start.19 = (f32[96]{0:T(128)S(1)}, f32[96]{0:T(128)}, u32[]{:S(2)}) copy-start(f32[96]{0:T(128)} %copy-done.18) | copy-start | bytes 1156
  219.9 291.9 %copy-start.21 = (f32[96]{0:T(128)S(1)}, f32[96]{0:T(128)}, u32[]{:S(2)}) copy-start(f32[96]{0:T(128)} %copy-done.20) | copy-start | bytes 1156
  219.9 291.9 %copy-start.23 = (f32[96]{0:T(128)S(1)}, f32[96]{0:T(128)}, u32[]{:S(2)}) copy-start(f32[96]{0:T(128)} %copy-done.22) | copy-start | bytes 1156
  219.9 291.9 %copy-start.25 = (f32[96]{0:T(128)S(1)}, f32[96]{0:T(128)}, u32[]{:S(2)}) copy-start(f32[96]{0:T(128)} %copy-done.24) | copy-start | bytes 1156
  219.9 291.9 %copy-start.27 = (f32[96]{0:T(128)S(1)}, f32[96]{0:T(128)}, u32[]{:S(2)}) copy-start(f32[96]{0:T(128)} %copy-done.26) | copy-start | bytes 1156
  219.9 291.9 %copy-start.29 = (f32[96]{0:T(128)S(1)}, f32[96]{0:T(128)}, u32[]{:S(2)}) copy-start(f32[96]{0:T(128)} %copy-done.28) | copy-start | bytes 1156
  219.9 291.9 %copy-start.31 = (f32[96]{0:T(128)S(1)}, f32[96]{0:T(128)}, u32[]{:S(2)}) copy-start(f32[96]{0:T(128)} %copy-done.30) | copy-start | bytes 1156
  219.9 291.9 %copy-start.33 = (f32[96]{0:T(128)S(1)}, f32[96]{0:T(128)}, u32[]{:S(2)}) copy-start(f32[96]{0:T(128)} %copy-done.32) | copy-start | bytes 1156
  220.0 291.9 %copy-start.35 = (f32[96]{0:T(128)S(1)}, f32[96]{0:T(128)}, u32[]{:S(2)}) copy-start(f32[96]{0:T(128)} %copy-done.34) | copy-start | bytes 1156
  220.0 291.9 %copy-start.37 = (f32[96]{0:T(128)S(1)}, f32[96]{0:T(128)}, u32[]{:S(2)}) copy-start(f32[96]{0:T(128)} %copy-done.36) | copy-start | bytes 1156
  220.0 291.9 %copy-start.39 = (f32[96]{0:T(128)S(1)}, f32[96]{0:T(128)}, u32[]{:S(2)}) copy-start(f32[96]{0:T(128)} %copy-done.38) | copy-start | bytes 1156
  220.0 291.9 %copy-start.41 = (f32[96]{0:T(128)S(1)}, f32[96]{0:T(128)}, u32[]{:S(2)}) copy-start(f32[96]{0:T(128)} %copy-done.40) | copy-start | bytes 1156
  220.0 291.9 %copy-start.43 = (f32[96]{0:T(128)S(1)}, f32[96]{0:T(128)}, u32[]{:S(2)}) copy-start(f32[96]{0:T(128)} %copy-done.42) | copy-start | bytes 1156
  220.0 291.9 %copy-start.45 = (f32[96]{0:T(128)S(1)}, f32[96]{0:T(128)}, u32[]{:S(2)}) copy-start(f32[96]{0:T(128)} %copy-done.44) | copy-start | bytes 1156
  220.0 291.9 %copy-start.47 = (f32[96]{0:T(128)S(1)}, f32[96]{0:T(128)}, u32[]{:S(2)}) copy-start(f32[96]{0:T(128)} %copy-done.46) | copy-start | bytes 1156
  220.0 291.9 %copy-start.49 = (f32[96]{0:T(128)S(1)}, f32[96]{0:T(128)}, u32[]{:S(2)}) copy-start(f32[96]{0:T(128)} %copy-done.48) | copy-start | bytes 1156
  220.0 291.9 %copy-start.51 = (f32[96]{0:T(128)S(1)}, f32[96]{0:T(128)}, u32[]{:S(2)}) copy-start(f32[96]{0:T(128)} %copy-done.50) | copy-start | bytes 1156
  220.0 291.9 %copy-start.53 = (f32[96]{0:T(128)S(1)}, f32[96]{0:T(128)}, u32[]{:S(2)}) copy-start(f32[96]{0:T(128)} %copy-done.52) | copy-start | bytes 1156
  220.1 291.9 %copy-start.55 = (f32[96]{0:T(128)S(1)}, f32[96]{0:T(128)}, u32[]{:S(2)}) copy-start(f32[96]{0:T(128)} %copy-done.54) | copy-start | bytes 1156
  220.1 291.9 %copy-start.57 = (f32[96]{0:T(128)S(1)}, f32[96]{0:T(128)}, u32[]{:S(2)}) copy-start(f32[96]{0:T(128)} %copy-done.56) | copy-start | bytes 1156
  220.1 291.9 %copy-start.59 = (f32[96]{0:T(128)S(1)}, f32[96]{0:T(128)}, u32[]{:S(2)}) copy-start(f32[96]{0:T(128)} %copy-done.58) | copy-start | bytes 1156
  220.1 291.9 %copy-start.61 = (f32[96]{0:T(128)S(1)}, f32[96]{0:T(128)}, u32[]{:S(2)}) copy-start(f32[96]{0:T(128)} %copy-done.60) | copy-start | bytes 1156
  220.1 291.9 %copy-start.63 = (f32[96]{0:T(128)S(1)}, f32[96]{0:T(128)}, u32[]{:S(2)}) copy-start(f32[96]{0:T(128)} %copy-done.62) | copy-start | bytes 1156
  220.1 291.9 %copy-start.65 = (f32[96]{0:T(128)S(1)}, f32[96]{0:T(128)}, u32[]{:S(2)}) copy-start(f32[96]{0:T(128)} %copy-done.64) | copy-start | bytes 1156
  220.1 291.9 %copy-start.67 = (f32[96]{0:T(128)S(1)}, f32[96]{0:T(128)}, u32[]{:S(2)}) copy-start(f32[96]{0:T(128)} %copy-done.66) | copy-start | bytes 1156
  220.1 291.9 %copy-start.69 = (f32[96]{0:T(128)S(1)}, f32[96]{0:T(128)}, u32[]{:S(2)}) copy-start(f32[96]{0:T(128)} %copy-done.68) | copy-start | bytes 1156
  220.1 291.9 %copy-start.71 = (f32[96]{0:T(128)S(1)}, f32[96]{0:T(128)}, u32[]{:S(2)}) copy-start(f32[96]{0:T(128)} %copy-done.70) | copy-start | bytes 1156
  220.1 291.9 %copy-start.73 = (f32[96]{0:T(128)S(1)}, f32[96]{0:T(128)}, u32[]{:S(2)}) copy-start(f32[96]{0:T(128)} %copy-done.72) | copy-start | bytes 1156
  220.2 291.9 %copy-start.75 = (f32[96]{0:T(128)S(1)}, f32[96]{0:T(128)}, u32[]{:S(2)}) copy-start(f32[96]{0:T(128)} %copy-done.74) | copy-start | bytes 1156
  220.2 291.9 %copy-start.77 = (f32[96]{0:T(128)S(1)}, f32[96]{0:T(128)}, u32[]{:S(2)}) copy-start(f32[96]{0:T(128)} %copy-done.76) | copy-start | bytes 1156
  220.2 291.9 %copy-start.79 = (f32[96]{0:T(128)S(1)}, f32[96]{0:T(128)}, u32[]{:S(2)}) copy-start(f32[96]{0:T(128)} %copy-done.78) | copy-start | bytes 1156
  220.2 291.9 %copy-start.81 = (f32[96]{0:T(128)S(1)}, f32[96]{0:T(128)}, u32[]{:S(2)}) copy-start(f32[96]{0:T(128)} %copy-done.80) | copy-start | bytes 1156
  220.3 290.8 %collective-permute-start.6 = (bf16[3,70,96]{1,0,2:T(4,128)(2,1)S(1)}, bf16[3,70,96]{1,0,2:T(4,128)(2,1)S(1)}, u32[]{:S(2)}, u32[]{:S(2)}) collective-permute-start(bf16[3,70,96]{1,0,2:T(4,128)(2,1)S(1)} %get-tuple-element.81), channel_id=1, source_target_pairs={{0,64},{8,72},{16,80},{24,88},{32,96},{40,104},{48,112},{56,120},{... | collective-permute-start | bytes 120968 | tf_op jit(solution)/shard_map/ppermute | solution.py:12
  226.7 284.3 %collective-permute-start.7 = (bf16[3,70,96]{1,0,2:T(4,128)(2,1)S(1)}, bf16[3,70,96]{1,0,2:T(4,128)(2,1)S(1)}, u32[]{:S(2)}, u32[]{:S(2)}) collective-permute-start(bf16[3,70,96]{1,0,2:T(4,128)(2,1)S(1)} %get-tuple-element.82), channel_id=1, source_target_pairs={{64,0},{72,8},{80,16},{88,24},{96,32},{104,40},{112,48},{120,56},{... | collective-permute-start | bytes 120968 | tf_op jit(solution)/shard_map/ppermute | solution.py:12
  (47 other events, 2227.8 us)
Sparse Core Ops, SparseCore 0:
  123.1 49.5 reduce-scatter.8
  175.5 42.9 reduce-scatter.6
Sparse Core Ops, SparseCore 1:
  130.4 574.7 all-reduce.4
where the time goes:
time: 717 us; the launch traced here: 716 us
  blocking collectives  374 us (52%)
  waiting for transfers between devices  231 us (32%)
  other arithmetic  46.2 us (6%)
  starting transfers between devices  26 us (4%)
  between operations  17.1 us (2%)
  local copies, waits for them, and re-layouts  16.4 us (2%)
    psum x1, blocking collectives, shards(): lax.psum((grad_in, grad_out, grad_kernel), 'sp')  282 us
    psum x1, waiting for transfers between devices, shards(): lax.psum((grad_in, grad_out, grad_kernel), 'sp')  180 us
    unnamed x5, waiting for transfers between devices  50.4 us
    all_gather x1, blocking collectives, shards(): grad_all = lax.all_gather(grad_map, 'ch', axis=2, tiled=True)  29.8 us
    all_gather x1, blocking collectives, shards(): lax.all_gather(((conv_f - mean) * rstd).astype(jnp.bfloat16), 'ch', axis=...  29.7 us
    ppermute x8, starting transfers between devices, passed_along(): return lax.ppermute(block, axis, route)  25.8 us
    reduce_sum x3, other arithmetic, shards(): jnp.sum(d_conv_f * padded[row:row + rows, col:col + cols], axis=(0, 1))  18.2 us
    psum x1, blocking collectives, shards(): lax.psum((jnp.sum(d_norm, axis=-1, keepdims=True), jnp.sum(d_norm * local...  16.5 us
  transfers between devices with their start and end apart: 11, of which 4 were waited for; matrix products, arithmetic and copies ran while one was open for 6% of the time, Pallas kernels for 0%

commit v1 on v0

--- a/solution.py
+++ b/solution.py
@@ -48,8 +48,14 @@
     mean = first_sum / chans
     var = square_sum / chans - mean * mean
     rstd = lax.rsqrt(var + 1e-06)
-    normed_all = lax.all_gather(
-        ((conv_f - mean) * rstd).astype(jnp.bfloat16), "ch", axis=2, tiled=True
+    normed_all = jnp.concatenate(
+        lax.all_to_all(
+            jnp.stack([((conv_f - mean) * rstd).astype(jnp.bfloat16)] * lax.axis_size("ch")),
+            "ch",
+            0,
+            0,
+        ),
+        axis=2,
     )
     local_hat = (conv_f - mean) * rstd
     pre = jnp.einsum("hwc,cf->hwf", normed_all, w_in, preferred_element_type=jnp.float32)

time: 717 us -> 684 us (0.954)
  other arithmetic: 46.2 us -> 7.19 us
  waiting for transfers between devices: 231 us -> 261 us
  blocking collectives: 374 us -> 345 us
  starting transfers between devices: 26 us -> 35.5 us
    all_gather x1 -> x0, blocking collectives: 29.7 us -> none  [shards(): lax.all_gather(((conv_f - mean) * rstd).astype(jnp.bfloat16), 'ch', axis=...]
    reduce_sum x3, other arithmetic: 18.2 us -> 1.05 us  [shards(): jnp.sum(d_conv_f * padded[row:row + rows, col:col + cols], axis=(0, 1))]
    unnamed x5, waiting for transfers between devices: 50.4 us -> 67.2 us
    ppermute x8, waiting for transfers between devices: 0.51 us -> 14.1 us  [passed_along(): return lax.ppermute(block, axis, route)]
    reduce_sum x1, other arithmetic: 12.5 us -> 1 us  [shards(): jnp.sum(conv_f, axis=-1, keepdims=True)]
    broadcast_in_dim x2, other arithmetic: 12.5 us -> 2.15 us  [shards(): return (output[None], grad_image[None], grad_in, grad_out, grad_kernel)]
    all_to_all x0 -> x1, starting transfers between devices: none -> 8.27 us  [shards(): lax.all_to_all(jnp.stack([((conv_f - mean) * rstd).astype(jnp.bfloat16)]...]
  transfers between devices with their start and end apart: 11 -> 12, of which waited for: 4 -> 7; matrix products, arithmetic and copies ran while one was open for 6% -> 2% of each run, Pallas kernels for 0% -> 0%
where the time goes in v1:
time: 684 us
  blocking collectives  345 us (50%)
  waiting for transfers between devices  261 us (38%)
  starting transfers between devices  35.5 us (5%)
  between operations  16.6 us (2%)
  local copies, waits for them, and re-layouts  13.7 us (2%)
  other arithmetic  7.19 us (1%)
    psum x1, blocking collectives, shards(): lax.psum((grad_in, grad_out, grad_kernel), 'sp')  282 us
    psum x1, waiting for transfers between devices, shards(): lax.psum((grad_in, grad_out, grad_kernel), 'sp')  179 us
    unnamed x5, waiting for transfers between devices  67.2 us
    all_gather x1, blocking collectives, shards(): grad_all = lax.all_gather(grad_map, 'ch', axis=2, tiled=True)  30 us
    ppermute x8, starting transfers between devices, passed_along(): return lax.ppermute(block, axis, route)  27.2 us
    psum x1, blocking collectives, shards(): lax.psum((jnp.sum(d_norm, axis=-1, keepdims=True), jnp.sum(d_norm * local...  16.4 us
    psum x1, blocking collectives, shards(): lax.psum((jnp.sum(conv_f, axis=-1, keepdims=True), jnp.sum(conv_f * conv_...  16.1 us
    ppermute x8, waiting for transfers between devices, passed_along(): return lax.ppermute(block, axis, route)  14.1 us
  transfers between devices with their start and end apart: 12, of which 7 were waited for; matrix products, arithmetic and copies ran while one was open for 2% of the time, Pallas kernels for 0%

profile of v1, /device:TPU:6, one launch (start us, length us, event | category | flops | bytes accessed | tf_op | source)
XLA Modules:
  0.0 683.6 jit_solution(18026066354694282077)
XLA Ops:
  8.0 0.8 fusion.126
  8.8 1.7 collective-permute-start
  10.5 1.3 collective-permute-start.1
  11.8 0.7 convert_element_type.55
  12.8 2.2 collective-permute-done.1
  15.0 0.9 pad_maximum_fusion
  15.9 9.7 %collective-permute-start.2 = (bf16[3,70,96]{2,1,0:T(8,128)(2,1)S(1)}, bf16[3,70,96]{2,1,0:T(8,128)(2,1)S(1)}, u32[]{:S(2)}, u32[]{:S(2)}) collective-permute-start(bf16[3,70,96]{2,1,0:T(8,128)(2,1)S(1)} %get-tuple-element.68), channel_id=1, source_target_pairs={{0,64},{8,72},{16,80},{24,88},{32,96},{40,104},{48,112},{56,120},{... | collective-permute-start | bytes 120968 | tf_op jit(solution)/shard_map/ppermute | solution.py:12
  25.5 1.3 collective-permute-start.3
  27.0 0.4 collective-permute-done.2
  27.3 8.2 %collective-permute-done.3 = bf16[3,70,96]{2,1,0:T(8,128)(2,1)S(1)} collective-permute-done((bf16[3,70,96]{2,1,0:T(8,128)(2,1)S(1)}, bf16[3,70,96]{2,1,0:T(8,128)(2,1)S(1)}, u32[]{:S(2)}, u32[]{:S(2)}) %collective-permute-start.3) | collective-permute-done | bytes 40352 | tf_op jit(solution)/shard_map/ppermute | solution.py:12
  35.5 0.9 maximum_convert_fusion
  36.5 1.0 convert_reduce_fusion.1
  37.6 16.1 %all-reduce.2 = (f32[4,64,1]{1,0,2:T(4,128)S(1)}, f32[4,64,1]{1,0,2:T(4,128)S(1)}) all-reduce(f32[4,64,1]{1,0,2:T(4,128)S(1)} %bitcast.206, f32[4,64,1]{1,0,2:T(4,128)S(1)} %bitcast.205), channel_id=1, replica_groups=mesh['sp'=64,'ch'=8] {'ch'}, use_global_device_ids=true, to_apply=%region_3.4 | all-reduce | flops 512 | bytes 4096 | tf_op jit(solution)/shard_map/psum | solution.py:44
  53.9 0.9 stack.161
  54.8 8.3 %all-to-all-start = ((bf16[8,4,64,96]{3,2,1,0:T(8,128)(2,1)}), bf16[8,4,64,96]{3,2,1,0:T(8,128)(2,1)S(1)}, u32[]{:S(2)}, u32[]{:S(2)}) async-start(bf16[8,4,64,96]{3,2,1,0:T(8,128)(2,1)} %stack.161), calls=%async_computation | async-start | bytes 1048576 | tf_op jit(solution)/shard_map/all_to_all | solution.py:52
  63.2 30.0 %all-gather = bf16[1,4,64,768]{2,1,0,3:T(4,128)(2,1)S(1)} all-gather(bf16[1,4,64,96]{2,1,0,3:T(4,128)(2,1)S(1)} %copy.11), channel_id=2, replica_groups=mesh['sp'=64,'ch'=8] {'ch'}, dimensions={3}, use_global_device_ids=true | all-gather | bytes 442368 | tf_op jit(solution)/shard_map/all_gather | solution.py:70
  93.2 0.5 copy.12
  93.8 0.3 copy.10
  94.1 0.4 reshape.22
  94.6 0.4 fusion.4
  95.2 0.4 fusion
  95.6 0.7 copy-done.2
  96.3 0.4 convolution_convert_fusion
  96.7 0.6 copy.15
  97.2 1.2 reshape.33
  98.6 1.4 convolution_convert_fusion.1
  100.0 0.6 copy.13
  100.6 1.2 reshape.31
  101.9 1.4 convolution_bitcast_fusion.1
  103.4 1.4 convolution_bitcast_fusion
  104.8 39.9 %reduce-scatter.9.cloned.1.call-done = bf16[96,256]{1,0:T(8,128)(2,1)} async-done(((bf16[768,256]{1,0:T(8,128)(2,1)}), bf16[96,256]{1,0:T(8,128)(2,1)}) %reduce-scatter.9.cloned.1.call-update) | async-done | bytes 49168
  144.7 0.9 reshape.34
  145.9 16.4 %all-reduce.1 = (f32[4,64]{1,0:T(4,128)S(1)}, f32[4,64,1]{1,0,2:T(4,128)S(1)}) all-reduce(f32[4,64]{1,0:T(4,128)S(1)} %get-tuple-element.55, f32[4,64,1]{1,0,2:T(4,128)S(1)} %bitcast.207), channel_id=1, replica_groups=mesh['sp'=64,'ch'=8] {'ch'}, use_global_device_ids=true, to_apply=%region_9.10 | all-reduce | flops 512 | bytes 4096 | tf_op jit(solution)/shard_map/psum | solution.py:84
  162.3 27.3 %reduce-scatter.7.cloned.1.call-done = bf16[96,256]{1,0:T(8,128)(2,1)} async-done(((bf16[768,256]{1,0:T(8,128)(2,1)}), bf16[96,256]{1,0:T(8,128)(2,1)}) %reduce-scatter.7.cloned.1.call-update) | async-done | bytes 49168
  189.6 0.9 reshape.32
  190.6 0.5 fusion.68
  191.1 1.3 collective-permute-start.4
  192.4 0.7 fusion.120
  193.1 0.3 fusion.69
  193.4 1.3 collective-permute-start.5
  194.7 3.4 collective-permute-done.5
  198.2 9.4 %collective-permute-start.6 = (bf16[3,70,96]{2,1,0:T(8,128)(2,1)S(1)}, bf16[3,70,96]{2,1,0:T(8,128)(2,1)S(1)}, u32[]{:S(2)}, u32[]{:S(2)}) collective-permute-start(bf16[3,70,96]{2,1,0:T(8,128)(2,1)S(1)} %get-tuple-element.66), channel_id=1, source_target_pairs={{0,64},{8,72},{16,80},{24,88},{32,96},{40,104},{48,112},{56,120},{... | collective-permute-start | bytes 120968 | tf_op jit(solution)/shard_map/ppermute | solution.py:12
  207.8 1.3 collective-permute-start.7
  209.5 282.1 %psum.55 = f32[7,7,96]{2,1,0:T(8,128)} all-reduce(f32[7,7,96]{2,1,0:T(8,128)S(1)} %reshape.23), channel_id=1, replica_groups=mesh['sp'=64,'ch'=8] {'sp'}, use_global_device_ids=true, to_apply=%region_61.62 | all-reduce | flops 4704 | bytes 37632 | tf_op jit(solution)/shard_map/psum | solution.py:107
  491.9 1.5 fusion.121
  493.4 179.2 %all-reduce.5.cloned.1.call-done = (f32[768,384]{1,0:T(8,128)}, f32[384,768]{1,0:T(8,128)}) async-done(((f32[768,384]{1,0:T(8,128)}, f32[384,768]{1,0:T(8,128)}), (f32[768,384]{1,0:T(8,128)}, f32[384,768]{1,0:T(8,128)})) %all-reduce.5.cloned.1.call-update) | async-done | bytes 2359312 | tf_op jit(solution)/shard_map/psum | solution.py:107
  672.7 2.5 copy.19
  675.1 1.0 copy.20
  (146 shorter events, 2.0 us)
Async XLA Ops:
  8.0 86.5 %copy-start = (bf16[768,384]{1,0:T(8,128)(2,1)S(1)}, bf16[768,384]{1,0:T(8,128)(2,1)}, u32[]{:S(2)}) copy-start(bf16[768,384]{1,0:T(8,128)(2,1)} %param.8) | copy-start | bytes 1769476
  8.8 3.9 collective-permute-start
  10.5 4.4 collective-permute-start.1
  12.6 23.8 %copy-start.7 = (f32[96]{0:T(128)}, f32[96]{0:T(128)S(1)}, u32[]{:S(2)}) copy-start(f32[96]{0:T(128)S(1)} %get-tuple-element.79) | copy-start | bytes 1156
  12.6 23.8 %copy-start.9 = (f32[96]{0:T(128)}, f32[96]{0:T(128)S(1)}, u32[]{:S(2)}) copy-start(f32[96]{0:T(128)S(1)} %get-tuple-element.80) | copy-start | bytes 1156
  12.6 23.8 %copy-start.11 = (f32[96]{0:T(128)}, f32[96]{0:T(128)S(1)}, u32[]{:S(2)}) copy-start(f32[96]{0:T(128)S(1)} %get-tuple-element.81) | copy-start | bytes 1156
  12.6 23.8 %copy-start.13 = (f32[96]{0:T(128)}, f32[96]{0:T(128)S(1)}, u32[]{:S(2)}) copy-start(f32[96]{0:T(128)S(1)} %get-tuple-element.82) | copy-start | bytes 1156
  12.6 23.8 %copy-start.15 = (f32[96]{0:T(128)}, f32[96]{0:T(128)S(1)}, u32[]{:S(2)}) copy-start(f32[96]{0:T(128)S(1)} %get-tuple-element.83) | copy-start | bytes 1156
  12.6 23.8 %copy-start.17 = (f32[96]{0:T(128)}, f32[96]{0:T(128)S(1)}, u32[]{:S(2)}) copy-start(f32[96]{0:T(128)S(1)} %get-tuple-element.84) | copy-start | bytes 1156
  12.6 23.8 %copy-start.19 = (f32[96]{0:T(128)}, f32[96]{0:T(128)S(1)}, u32[]{:S(2)}) copy-start(f32[96]{0:T(128)S(1)} %get-tuple-element.85) | copy-start | bytes 1156
  12.7 23.8 %copy-start.21 = (f32[96]{0:T(128)}, f32[96]{0:T(128)S(1)}, u32[]{:S(2)}) copy-start(f32[96]{0:T(128)S(1)} %get-tuple-element.86) | copy-start | bytes 1156
  12.7 23.8 %copy-start.23 = (f32[96]{0:T(128)}, f32[96]{0:T(128)S(1)}, u32[]{:S(2)}) copy-start(f32[96]{0:T(128)S(1)} %get-tuple-element.87) | copy-start | bytes 1156
  15.9 11.5 %collective-permute-start.2 = (bf16[3,70,96]{2,1,0:T(8,128)(2,1)S(1)}, bf16[3,70,96]{2,1,0:T(8,128)(2,1)S(1)}, u32[]{:S(2)}, u32[]{:S(2)}) collective-permute-start(bf16[3,70,96]{2,1,0:T(8,128)(2,1)S(1)} %get-tuple-element.68), channel_id=1, source_target_pairs={{0,64},{8,72},{16,80},{24,88},{32,96},{40,104},{48,112},{56,120},{... | collective-permute-start | bytes 120968 | tf_op jit(solution)/shard_map/ppermute | solution.py:12
  25.5 10.0 %collective-permute-start.3 = (bf16[3,70,96]{2,1,0:T(8,128)(2,1)S(1)}, bf16[3,70,96]{2,1,0:T(8,128)(2,1)S(1)}, u32[]{:S(2)}, u32[]{:S(2)}) collective-permute-start(bf16[3,70,96]{2,1,0:T(8,128)(2,1)S(1)} %get-tuple-element.69), channel_id=1, source_target_pairs={{64,0},{72,8},{80,16},{88,24},{96,32},{104,40},{112,48},{120,56},{... | collective-permute-start | bytes 120968 | tf_op jit(solution)/shard_map/ppermute | solution.py:12
  37.6 25.5 %copy-start.6 = (bf16[1,4,64,96]{3,2,1,0:T(8,128)(2,1)S(1)}, bf16[1,4,64,96]{3,2,1,0:T(8,128)(2,1)}, u32[]{:S(2)}) copy-start(bf16[1,4,64,96]{3,2,1,0:T(8,128)(2,1)} %param.6) | copy-start | bytes 147460
  54.8 38.9 %all-to-all-start = ((bf16[8,4,64,96]{3,2,1,0:T(8,128)(2,1)}), bf16[8,4,64,96]{3,2,1,0:T(8,128)(2,1)S(1)}, u32[]{:S(2)}, u32[]{:S(2)}) async-start(bf16[8,4,64,96]{3,2,1,0:T(8,128)(2,1)} %stack.161), calls=%async_computation | async-start | bytes 1048576 | tf_op jit(solution)/shard_map/all_to_all | solution.py:52
  63.1 81.5 %reduce-scatter.9.cloned.1.call-start = ((), (), s32[]{:S(2)}) async-start(), calls=%async_computation.4 | async-start | bytes 442368
  98.5 91.1 %reduce-scatter.7.cloned.1.call-start = ((), (), s32[]{:S(2)}) async-start(), calls=%async_computation.3 | async-start | bytes 442368
  101.9 570.8 %all-reduce.5.cloned.1.call-start = ((), (), s32[]{:S(2)}) async-start(), calls=%async_computation.5 | async-start | bytes 4718592 | tf_op jit(solution)/shard_map/psum | solution.py:107
  191.1 3.6 collective-permute-start.4
  193.4 4.7 collective-permute-start.5
  198.2 293.4 %collective-permute-start.6 = (bf16[3,70,96]{2,1,0:T(8,128)(2,1)S(1)}, bf16[3,70,96]{2,1,0:T(8,128)(2,1)S(1)}, u32[]{:S(2)}, u32[]{:S(2)}) collective-permute-start(bf16[3,70,96]{2,1,0:T(8,128)(2,1)S(1)} %get-tuple-element.66), channel_id=1, source_target_pairs={{0,64},{8,72},{16,80},{24,88},{32,96},{40,104},{48,112},{56,120},{... | collective-permute-start | bytes 120968 | tf_op jit(solution)/shard_map/ppermute | solution.py:12
  207.5 284.1 %copy-start.8 = (f32[96]{0:T(128)S(1)}, f32[96]{0:T(128)}, u32[]{:S(2)}) copy-start(f32[96]{0:T(128)} %copy-done.7) | copy-start | bytes 1156
  207.6 284.1 %copy-start.10 = (f32[96]{0:T(128)S(1)}, f32[96]{0:T(128)}, u32[]{:S(2)}) copy-start(f32[96]{0:T(128)} %copy-done.9) | copy-start | bytes 1156
  207.6 284.1 %copy-start.12 = (f32[96]{0:T(128)S(1)}, f32[96]{0:T(128)}, u32[]{:S(2)}) copy-start(f32[96]{0:T(128)} %copy-done.11) | copy-start | bytes 1156
  207.6 284.1 %copy-start.14 = (f32[96]{0:T(128)S(1)}, f32[96]{0:T(128)}, u32[]{:S(2)}) copy-start(f32[96]{0:T(128)} %copy-done.13) | copy-start | bytes 1156
  207.6 284.1 %copy-start.16 = (f32[96]{0:T(128)S(1)}, f32[96]{0:T(128)}, u32[]{:S(2)}) copy-start(f32[96]{0:T(128)} %copy-done.15) | copy-start | bytes 1156
  207.6 284.1 %copy-start.18 = (f32[96]{0:T(128)S(1)}, f32[96]{0:T(128)}, u32[]{:S(2)}) copy-start(f32[96]{0:T(128)} %copy-done.17) | copy-start | bytes 1156
  207.6 284.1 %copy-start.20 = (f32[96]{0:T(128)S(1)}, f32[96]{0:T(128)}, u32[]{:S(2)}) copy-start(f32[96]{0:T(128)} %copy-done.19) | copy-start | bytes 1156
  207.6 284.1 %copy-start.22 = (f32[96]{0:T(128)S(1)}, f32[96]{0:T(128)}, u32[]{:S(2)}) copy-start(f32[96]{0:T(128)} %copy-done.21) | copy-start | bytes 1156
  207.6 284.1 %copy-start.24 = (f32[96]{0:T(128)S(1)}, f32[96]{0:T(128)}, u32[]{:S(2)}) copy-start(f32[96]{0:T(128)} %copy-done.23) | copy-start | bytes 1156
  207.6 284.1 %copy-start.26 = (f32[96]{0:T(128)S(1)}, f32[96]{0:T(128)}, u32[]{:S(2)}) copy-start(f32[96]{0:T(128)} %copy-done.25) | copy-start | bytes 1156
  207.7 284.1 %copy-start.28 = (f32[96]{0:T(128)S(1)}, f32[96]{0:T(128)}, u32[]{:S(2)}) copy-start(f32[96]{0:T(128)} %copy-done.27) | copy-start | bytes 1156
  207.7 284.1 %copy-start.30 = (f32[96]{0:T(128)S(1)}, f32[96]{0:T(128)}, u32[]{:S(2)}) copy-start(f32[96]{0:T(128)} %copy-done.29) | copy-start | bytes 1156
  207.7 284.1 %copy-start.32 = (f32[96]{0:T(128)S(1)}, f32[96]{0:T(128)}, u32[]{:S(2)}) copy-start(f32[96]{0:T(128)} %copy-done.31) | copy-start | bytes 1156
  207.7 284.1 %copy-start.34 = (f32[96]{0:T(128)S(1)}, f32[96]{0:T(128)}, u32[]{:S(2)}) copy-start(f32[96]{0:T(128)} %copy-done.33) | copy-start | bytes 1156
  207.7 284.1 %copy-start.36 = (f32[96]{0:T(128)S(1)}, f32[96]{0:T(128)}, u32[]{:S(2)}) copy-start(f32[96]{0:T(128)} %copy-done.35) | copy-start | bytes 1156
  207.7 284.1 %copy-start.38 = (f32[96]{0:T(128)S(1)}, f32[96]{0:T(128)}, u32[]{:S(2)}) copy-start(f32[96]{0:T(128)} %copy-done.37) | copy-start | bytes 1156
  207.7 284.1 %copy-start.40 = (f32[96]{0:T(128)S(1)}, f32[96]{0:T(128)}, u32[]{:S(2)}) copy-start(f32[96]{0:T(128)} %copy-done.39) | copy-start | bytes 1156
  207.7 284.1 %copy-start.42 = (f32[96]{0:T(128)S(1)}, f32[96]{0:T(128)}, u32[]{:S(2)}) copy-start(f32[96]{0:T(128)} %copy-done.41) | copy-start | bytes 1156
  207.7 284.1 %copy-start.44 = (f32[96]{0:T(128)S(1)}, f32[96]{0:T(128)}, u32[]{:S(2)}) copy-start(f32[96]{0:T(128)} %copy-done.43) | copy-start | bytes 1156
  207.7 284.1 %copy-start.46 = (f32[96]{0:T(128)S(1)}, f32[96]{0:T(128)}, u32[]{:S(2)}) copy-start(f32[96]{0:T(128)} %copy-done.45) | copy-start | bytes 1156
  207.8 284.1 %copy-start.48 = (f32[96]{0:T(128)S(1)}, f32[96]{0:T(128)}, u32[]{:S(2)}) copy-start(f32[96]{0:T(128)} %copy-done.47) | copy-start | bytes 1156
  207.8 284.1 %copy-start.50 = (f32[96]{0:T(128)S(1)}, f32[96]{0:T(128)}, u32[]{:S(2)}) copy-start(f32[96]{0:T(128)} %copy-done.49) | copy-start | bytes 1156
  207.8 284.1 %copy-start.52 = (f32[96]{0:T(128)S(1)}, f32[96]{0:T(128)}, u32[]{:S(2)}) copy-start(f32[96]{0:T(128)} %copy-done.51) | copy-start | bytes 1156
  207.8 284.1 %copy-start.54 = (f32[96]{0:T(128)S(1)}, f32[96]{0:T(128)}, u32[]{:S(2)}) copy-start(f32[96]{0:T(128)} %copy-done.53) | copy-start | bytes 1156
  207.8 284.1 %copy-start.56 = (f32[96]{0:T(128)S(1)}, f32[96]{0:T(128)}, u32[]{:S(2)}) copy-start(f32[96]{0:T(128)} %copy-done.55) | copy-start | bytes 1156
  207.8 283.8 %collective-permute-start.7 = (bf16[3,70,96]{2,1,0:T(8,128)(2,1)S(1)}, bf16[3,70,96]{2,1,0:T(8,128)(2,1)S(1)}, u32[]{:S(2)}, u32[]{:S(2)}) collective-permute-start(bf16[3,70,96]{2,1,0:T(8,128)(2,1)S(1)} %get-tuple-element.67), channel_id=1, source_target_pairs={{64,0},{72,8},{80,16},{88,24},{96,32},{104,40},{112,48},{120,56},{... | collective-permute-start | bytes 120968 | tf_op jit(solution)/shard_map/ppermute | solution.py:12
  (21 other events, 241.6 us)
Sparse Core Ops, SparseCore 0:
  98.6 45.9 reduce-scatter.8
  147.5 42.1 reduce-scatter.6
Sparse Core Ops, SparseCore 1:
  105.9 566.7 all-reduce.4
